TPU v7x, 128 devices: a whole 4x4x4 slice. The times are simulated.
128 devices in a mesh: seq: 8 (over y, core), vocab: 16 (over x, z).
Axes of the slice: x: 4, y: 4, z: 4, core: 2. Of those that a mesh axis runs over, the one named last changes fastest.
Arguments:
- queries: bfloat16 [8192, 2, 2048], P(('seq', 'vocab')), may hold values from -40 to 40
- key_vectors: bfloat16 [8192, 2, 2048], P(('seq', 'vocab')), may hold values from -40 to 40
- value_vectors: bfloat16 [8192, 2, 2048], P(('seq', 'vocab')), may hold values from -18 to 18
- residual: bfloat16 [8192, 2, 2048], P(('seq', 'vocab')), may hold values from -3 to 3
- norm_gain: float32 [2048], replicated, may hold values from 0.1 to 1.9
- head_weight: bfloat16 [2048, 16384], P(None, 'vocab'), may hold values from -0.125 to 0.125
- head_bias: float32 [16384], P('vocab'), may hold values from -6 to 6
- doc_lengths: int32 [2], replicated, may hold values from 1 to 8192, 12288 in all
Outputs:
- pooled: float32 [2, 16384], P(None, 'vocab')
- grad_hidden: bfloat16 [8192, 2, 2048], P(('seq', 'vocab'))
Inputs may be any that keep to these rules, and one draw needn't show every extreme that they name: `doc_lengths`: the lengths add up to 12288.
All inputs are finite; a program needn't handle non-finite values.
Results may differ from a plain program's by a relative error of at most 0.018.
Values may be sent and summed in bfloat16 or wider, within the bound.
No kernel may reach another device: no remote copies, remote signals or barrier semaphores. Data moves between devices by JAX's collectives and lax.ppermute only.
A program may use at most 128 MiB of HBM per device.

v0:
```python
import math
import jax
import jax.numpy as jnp
from jax import lax
from jax.sharding import PartitionSpec as P

HEAD_DIM = 128
sharpness = 8.0
flops_weight = 500.0
epsilon = 1e-05


def local(
    queries, key_vectors, value_vectors, residual, norm_gain, head_weight, head_bias, doc_lengths
):
    tokens_here = queries.shape[0]
    docs_count = queries.shape[1]
    vocab_count = lax.axis_size("vocab")
    seq_at = lax.axis_index("seq")
    query_heads, key_heads, value_heads = (
        lax.all_to_all(queries, "seq", split_axis=2, concat_axis=0, tiled=True),
        lax.all_to_all(key_vectors, "seq", split_axis=2, concat_axis=0, tiled=True),
        lax.all_to_all(value_vectors, "seq", split_axis=2, concat_axis=0, tiled=True),
    )
    block_rows = query_heads.shape[0]
    local_width = query_heads.shape[2]
    local_heads = local_width // HEAD_DIM
    query_split = query_heads.reshape(block_rows, docs_count, local_heads, HEAD_DIM)
    within = jnp.arange(block_rows, dtype=jnp.int32)

    def attend_block(carry, block):
        highest, total, summed = carry
        key_block, value_block, shard = block
        key_split = key_block.reshape(block_rows, docs_count, local_heads, HEAD_DIM)
        value_split = value_block.reshape(block_rows, docs_count, local_heads, HEAD_DIM)
        key_place = (
            within // tokens_here * vocab_count + shard
        ) * tokens_here + within % tokens_here
        allowed = (key_place[None, :] < doc_lengths[:, None])[:, None, None, :]
        scores = jnp.einsum(
            "qbhe,kbhe->bhqk", query_split, key_split, preferred_element_type=jnp.float32
        ) / math.sqrt(HEAD_DIM)
        block_top = jnp.max(jnp.where(allowed, scores, -1e30), axis=3)
        new_top = jnp.maximum(highest, block_top)
        weights = jnp.where(allowed, jnp.exp(scores - new_top[..., None]), 0.0)
        shrink = jnp.exp(highest - new_top)
        total = total * shrink + jnp.sum(weights, axis=3)
        added = jnp.einsum(
            "bhqk,kbhe->qbhe",
            weights.astype(jnp.bfloat16),
            value_split,
            preferred_element_type=jnp.float32,
        )
        summed = summed * jnp.transpose(shrink, (2, 0, 1))[..., None] + added
        return ((new_top, total, summed), None)

    initial = (
        jnp.full((docs_count, local_heads, block_rows), -1e30, jnp.float32),
        jnp.zeros((docs_count, local_heads, block_rows), jnp.float32),
        jnp.zeros((block_rows, docs_count, local_heads, HEAD_DIM), jnp.float32),
    )
    carry = initial
    key_piece = lax.all_gather(key_heads, "vocab", axis=0, tiled=True)
    value_piece = lax.all_gather(value_heads, "vocab", axis=0, tiled=True)
    count = key_piece.shape[0] // block_rows
    key_blocks = key_piece.reshape(count, block_rows, docs_count, local_width)
    value_blocks = value_piece.reshape(count, block_rows, docs_count, local_width)
    shards = jnp.arange(count, dtype=jnp.int32)
    carry, unused = lax.scan(attend_block, carry, (key_blocks, value_blocks, shards))
    highest, total, summed = carry
    attended = (
        (summed / jnp.transpose(total, (2, 0, 1))[..., None])
        .reshape(block_rows, docs_count, local_width)
        .astype(jnp.bfloat16)
    )
    returned = lax.all_to_all(attended, "seq", split_axis=0, concat_axis=2, tiled=True)
    combined = residual.astype(jnp.float32) + returned.astype(jnp.float32)
    inv_rms = lax.rsqrt(jnp.mean(combined * combined, axis=2, keepdims=True) + epsilon)
    hidden = (combined * inv_rms * norm_gain).astype(jnp.bfloat16)
    arrived = lax.all_gather(hidden, "vocab", axis=0, tiled=True)
    row_count = arrived.shape[0]
    flattened = jnp.dot(
        arrived.reshape(row_count * docs_count, arrived.shape[2]),
        head_weight,
        preferred_element_type=jnp.float32,
    )
    logits = flattened.reshape(row_count, docs_count, head_weight.shape[1]) + head_bias
    gathered_rows = logits.shape[0]
    row_index = jnp.arange(gathered_rows, dtype=jnp.int32)
    position = (
        seq_at * vocab_count + row_index // tokens_here
    ) * tokens_here + row_index % tokens_here
    row_allowed = position[:, None] < doc_lengths[None, :]
    saturated = jnp.log1p(jnp.maximum(logits, 0.0))
    boosted = jnp.where(row_allowed[:, :, None], jnp.exp(sharpness * saturated), 0.0)
    partial_sums = jnp.sum(boosted, axis=0)
    lengths_float = doc_lengths[:, None].astype(jnp.float32)
    totals = lax.psum(partial_sums, "seq")
    pooled = jnp.log(totals / lengths_float) / sharpness
    coefficient = 2.0 * flops_weight / docs_count * jnp.mean(pooled, axis=0)[None, :] / totals
    derivative = jnp.where(logits > 0.0, 1.0 / (1.0 + jnp.maximum(logits, 0.0)), 0.0)
    dlogits = (coefficient[None, :, :] * boosted * derivative).astype(jnp.bfloat16)
    flattened = lax.dot_general(
        dlogits.reshape(gathered_rows * docs_count, dlogits.shape[2]),
        head_weight,
        (((1,), (1,)), ((), ())),
        preferred_element_type=jnp.float32,
    )
    own_rows = lax.psum_scatter(
        flattened.reshape(gathered_rows, docs_count, head_weight.shape[0]).astype(jnp.bfloat16),
        "vocab",
        scatter_dimension=0,
        tiled=True,
    )
    return (pooled, own_rows)


def solution(mesh):
    in_specs = (
        P(("seq", "vocab"), None, None),
        P(("seq", "vocab"), None, None),
        P(("seq", "vocab"), None, None),
        P(("seq", "vocab"), None, None),
        P(),
        P(None, "vocab"),
        P("vocab"),
        P(),
    )
    out_specs = (P(None, "vocab"), P(("seq", "vocab"), None, None))
    return jax.shard_map(local, mesh=mesh, in_specs=in_specs, out_specs=out_specs, check_vma=False)
```

profile of v0, /device:TPU:0, one launch (start us, length us, event | category | flops | bytes accessed | tf_op | source)
XLA Modules:
  0.0 576.1 jit_solution(2232000277719809404)
XLA Ops:
  7.2 2.6 copy.75
  10.6 14.7 %all_to_all.60 = bf16[8,2,16384]{2,1,0:T(2,128)(2,1)S(1)} all-to-all(bf16[8,2,16384]{2,1,0:T(2,128)(2,1)S(1)} %reshape.212), channel_id=1, replica_groups=mesh['seq'=8,'vocab'=16] {'seq'}, dimensions={0} | all-to-all | bytes 1048576 | tf_op jit(solution)/shard_map/all_to_all | solution.py:23
  27.9 2.6 copy.70
  31.2 12.8 %all_to_all.61 = bf16[8,2,16384]{2,1,0:T(2,128)(2,1)S(1)} all-to-all(bf16[8,2,16384]{2,1,0:T(2,128)(2,1)S(1)} %reshape.208), channel_id=1, replica_groups=mesh['seq'=8,'vocab'=16] {'seq'}, dimensions={0} | all-to-all | bytes 1048576 | tf_op jit(solution)/shard_map/all_to_all | solution.py:22
  49.0 3.5 all-to-all-start.1
  52.6 10.2 %all-to-all-done.1 = bf16[8,2,16384]{2,1,0:T(2,128)(2,1)S(1)} async-done(((bf16[8,2,16384]{2,1,0:T(2,128)(2,1)}), bf16[8,2,16384]{2,1,0:T(2,128)(2,1)S(1)}, u32[]{:S(2)}, u32[]{:S(2)}) %all-to-all-start.1) | async-done | bytes 524320 | tf_op jit(solution)/shard_map/all_to_all | solution.py:21
  64.3 35.0 %all-gather.6.cloned.1.call-done = bf16[8192,2,256]{2,0,1:T(8,128)(2,1)} async-done(((bf16[512,2,256]{2,0,1:T(8,128)(2,1)}), bf16[8192,2,256]{2,0,1:T(8,128)(2,1)}) %all-gather.6.cloned.1.call-update) | async-done | bytes 8388624 | tf_op jit(solution)/shard_map/all_gather | solution.py:64
  99.3 73.3 %all-gather.4.cloned.1.call-done = bf16[8192,2,256]{2,0,1:T(8,128)(2,1)} async-done(((bf16[512,2,256]{2,0,1:T(8,128)(2,1)}), bf16[8192,2,256]{2,0,1:T(8,128)(2,1)}) %all-gather.4.cloned.1.call-update) | async-done | bytes 8388624 | tf_op jit(solution)/shard_map/all_gather | solution.py:63
  172.6 168.6 %while.20 = (s32[]{:T(128)}, f32[2,2,512]{2,1,0:T(2,128)S(1)}, f32[2,2,512]{2,1,0:T(2,128)S(1)}, f32[512,2,2,128]{0,3,2,1:T(8,128)S(1)}, s32[16]{0:T(128)S(1)}, ...) while((s32[]{:T(128)}, f32[2,2,512]{2,1,0:T(2,128)S(1)}, ...), condition=%wide.region_3.4_spmd.clone.clone, body=%wide.region_0.3_spmd.clone.clone.sunk | while | flops 549213184 | bytes 37364912 | solution.py:69
  175.5 3.0 select_reduce_fusion.2
  178.7 3.5 fusion.75
  186.0 3.0 select_reduce_fusion.2
  189.3 3.5 fusion.75
  196.5 3.0 select_reduce_fusion.2
  199.8 3.5 fusion.75
  207.1 3.0 select_reduce_fusion.2
  210.3 3.5 fusion.75
  217.6 3.0 select_reduce_fusion.2
  220.9 3.5 fusion.75
  228.2 3.0 select_reduce_fusion.2
  231.4 3.5 fusion.75
  238.7 3.0 select_reduce_fusion.2
  241.9 3.5 fusion.75
  249.2 3.0 select_reduce_fusion.2
  252.5 3.5 fusion.75
  259.8 3.0 select_reduce_fusion.2
  263.0 3.5 fusion.75
  270.3 3.0 select_reduce_fusion.2
  273.5 3.5 fusion.75
  280.8 3.0 select_reduce_fusion.2
  284.1 3.5 fusion.75
  291.4 3.0 select_reduce_fusion.2
  294.6 3.5 fusion.75
  301.9 3.0 select_reduce_fusion.2
  305.2 3.5 fusion.75
  312.4 3.0 select_reduce_fusion.2
  315.7 3.5 fusion.75
  323.0 3.0 select_reduce_fusion.2
  326.2 3.5 fusion.75
  333.5 3.0 select_reduce_fusion.2
  336.8 3.5 fusion.75
  341.8 14.4 %all_to_all.62 = bf16[512,2,256]{2,1,0:T(2,128)(2,1)S(1)} all-to-all(bf16[512,2,256]{2,1,0:T(2,128)(2,1)S(1)} %copy.91), channel_id=1, replica_groups=mesh['seq'=8,'vocab'=16] {'seq'}, dimensions={0} | all-to-all | bytes 1048576 | tf_op jit(solution)/shard_map/all_to_all | solution.py:76
  358.3 68.5 %all-gather.8.cloned.1.call-done = bf16[1024,2,2048]{2,0,1:T(8,128)(2,1)} async-done(((bf16[64,2,2048]{2,0,1:T(8,128)(2,1)}), bf16[1024,2,2048]{2,0,1:T(8,128)(2,1)}) %all-gather.8.cloned.1.call-update) | async-done | bytes 8388624 | tf_op jit(solution)/shard_map/all_gather | solution.py:80
  426.8 17.6 %fusion.29 = (f32[2,1024]{1,0:T(2,128)S(1)}, f32[1024,2,1024]{2,0,1:T(8,128)}) fusion(f32[1024]{0:T(1024)S(1)} %copy-done.6, pred[1024,2]{0,1:T(4,128)(4,1)S(1)} %broadcast_compare_fusion.1, bf16[1024,2,2048]{2,0,1:T(8,128)(2,1)} %all-gather.8.cloned.1.call-done, bf16[2048,1024]{1,0:T(8,128)(2,1)} %param.15), kind=kOutput, calls=%fused_computation.44 | convolution fusion | flops 8600418304 | bytes 20985856 | tf_op jit(solution)/shard_map/dot_general | solution.py:82
  444.4 14.7 %psum.7 = f32[2,1024]{1,0:T(2,128)S(1)} all-reduce(f32[2,1024]{1,0:T(2,128)S(1)} %get-tuple-element.387), channel_id=1, replica_groups=mesh['seq'=8,'vocab'=16] {'seq'}, use_global_device_ids=true, to_apply=%region_6.7 | all-reduce | flops 2048 | bytes 16384 | tf_op jit(solution)/shard_map/psum | solution.py:98
  459.8 5.2 fusion.40
  465.0 19.0 %convolution_convert_fusion = bf16[1024,2,2048]{2,0,1:T(8,128)(2,1)} fusion(f32[1024,2,1024]{2,0,1:T(8,128)S(1)} %copy-done.1, bf16[2048,1024]{1,0:T(8,128)(2,1)} %param.15, f32[2,1024]{1,0:T(2,128)S(1)} %broadcast_divide_fusion, f32[1024]{0:T(1024)S(1)} %copy-done.6, pred[1024,2]{0,1:T(4,128)(4,1)S(1)} %broadcast_compare_fusion.1, ...), kind=kOutput, calls=%fused_computation.45 | convolution fusion | flops 8623489024 | bytes 22034432 | tf_op jit(solution)/shard_map/dot_general | solution.py:103
  483.9 83.3 %reduce-scatter.2.cloned.1.call-done = bf16[64,2,2048]{2,0,1:T(8,128)(2,1)} async-done(((bf16[1024,2,2048]{2,0,1:T(8,128)(2,1)}), bf16[64,2,2048]{2,0,1:T(8,128)(2,1)}) %reduce-scatter.2.cloned.1.call-update) | async-done | bytes 524304 | tf_op jit(solution)/shard_map/reduce_scatter | solution.py:109
  (259 shorter events, 80.0 us)
Async XLA Ops:
  7.2 39.4 %copy-start.3 = (bf16[64,2,2048]{2,1,0:T(2,128)(2,1)S(1)}, bf16[64,2,2048]{2,1,0:T(2,128)(2,1)}, u32[]{:S(2)}) copy-start(bf16[64,2,2048]{2,1,0:T(2,128)(2,1)} %param.10) | copy-start | bytes 1572868
  7.2 92.1 %all-gather.6.cloned.1.call-start = ((), (), s32[]{:S(2)}) async-start(), calls=%async_computation.6 | async-start | bytes 8912896 | tf_op jit(solution)/shard_map/all_gather | solution.py:64
  27.9 144.8 %copy-start.4 = (s32[2]{0:T(128)S(1)}, s32[2]{0:T(128)}, u32[]{:S(2)}) copy-start(s32[2]{0:T(128)} %param.17) | copy-start | bytes 28
  27.9 144.8 %all-gather.4.cloned.1.call-start = ((), (), s32[]{:S(2)}) async-start(), calls=%async_computation.5 | async-start | bytes 8912896 | tf_op jit(solution)/shard_map/all_gather | solution.py:63
  49.0 13.7 %all-to-all-start.1 = ((bf16[8,2,16384]{2,1,0:T(2,128)(2,1)}), bf16[8,2,16384]{2,1,0:T(2,128)(2,1)S(1)}, u32[]{:S(2)}, u32[]{:S(2)}) async-start(bf16[8,2,16384]{2,1,0:T(2,128)(2,1)} %reshape.210), calls=%async_computation.1 | async-start | bytes 1048576 | tf_op jit(solution)/shard_map/all_to_all | solution.py:21
  52.5 374.3 %all-gather.8.cloned.1.call-start = ((), (), s32[]{:S(2)}) async-start(), calls=%async_computation.7 | async-start | bytes 8912896 | tf_op jit(solution)/shard_map/all_gather | solution.py:80
  178.7 3.5 copy-start
  189.3 3.5 copy-start
  199.8 3.5 copy-start
  210.3 3.5 copy-start
  220.9 3.5 copy-start
  231.4 3.5 copy-start
  241.9 3.5 copy-start
  252.5 3.5 copy-start
  263.0 3.5 copy-start
  273.5 3.5 copy-start
  284.1 3.5 copy-start
  294.6 3.5 copy-start
  305.1 3.5 copy-start
  315.7 3.5 copy-start
  326.2 3.5 copy-start
  336.7 3.5 copy-start
  341.2 15.4 %copy-start.2 = (bf16[64,2,2048]{2,1,0:T(2,128)(2,1)S(1)}, bf16[64,2,2048]{2,1,0:T(2,128)(2,1)}, u32[]{:S(2)}) copy-start(bf16[64,2,2048]{2,1,0:T(2,128)(2,1)} %param.13) | copy-start | bytes 1572868
  341.2 15.7 %copy-start.5 = (f32[2048]{0:T(1024)S(1)}, f32[2048]{0:T(1024)}, u32[]{:S(2)}) copy-start(f32[2048]{0:T(1024)} %param.14) | copy-start | bytes 24580
  341.2 85.6 %copy-start.6 = (f32[1024]{0:T(1024)S(1)}, f32[1024]{0:T(1024)}, u32[]{:S(2)}) copy-start(f32[1024]{0:T(1024)} %param.16) | copy-start | bytes 12292
  358.0 209.2 %reduce-scatter.2.cloned.1.call-start = ((), (), s32[]{:S(2)}) async-start(), calls=%async_computation.8 | async-start | bytes 8912896 | tf_op jit(solution)/shard_map/reduce_scatter | solution.py:109
  459.1 5.9 %copy-start.1 = (f32[1024,2,1024]{2,0,1:T(8,128)S(1)}, f32[1024,2,1024]{2,0,1:T(8,128)}, u32[]{:S(2)}) copy-start(f32[1024,2,1024]{2,0,1:T(8,128)} %get-tuple-element.388) | copy-start | bytes 25165828
Sparse Core Ops, SparseCore 0:
  28.0 71.2 all-gather.5
  102.1 70.5 all-gather.3
  358.1 68.6 all-gather.7
  484.0 83.1 reduce-scatter.1
where the time goes:
time: 577 us; the launch traced here: 576 us
  waiting for transfers between devices  270 us (47%)
  matrix products  140 us (24%)
  blocking collectives  56.6 us (10%)
  local copies, waits for them, and re-layouts  55.2 us (10%)
  other arithmetic  34.8 us (6%)
  between operations  14 us (2%)
    reduce_scatter x1, waiting for transfers between devices, local(): lax.psum_scatter(flattened.reshape(gathered_rows, docs_count, head_weight...  83.3 us
    all_gather x1, waiting for transfers between devices, local(): key_piece = lax.all_gather(key_heads, 'vocab', axis=0, tiled=True)  73.3 us
    all_gather x1, waiting for transfers between devices, local(): arrived = lax.all_gather(hidden, 'vocab', axis=0, tiled=True)  68.5 us
    dot_general x16, matrix products, attend_block(): jnp.einsum('bhqk,kbhe->qbhe', weights.astype(jnp.bfloat16), value_split,...  55.5 us
    dot_general x16, matrix products, attend_block(): jnp.einsum('qbhe,kbhe->bhqk', query_split, key_split, preferred_element_t...  48.2 us
    dynamic_slice x64, local copies, waits for them, and re-layouts, local(): lax.scan(attend_block, carry, (key_blocks, value_blocks, shards))  36.4 us
    all_gather x1, waiting for transfers between devices, local(): value_piece = lax.all_gather(value_heads, 'vocab', axis=0, tiled=True)  35 us
    dot_general x1, matrix products, local(): lax.dot_general(dlogits.reshape(gathered_rows * docs_count, dlogits.shape...  19 us
  transfers between devices with their start and end apart: 5, of which 5 were waited for; matrix products, arithmetic and copies ran while one was open for 2% of the time, Pallas kernels for 0%

commit v1 on v0

--- a/solution.py
+++ b/solution.py
@@ -3,6 +3,7 @@
 import jax.numpy as jnp
 from jax import lax
 from jax.sharding import PartitionSpec as P
+from jax.lax import all_to_all, psum
 
 HEAD_DIM = 128
 sharpness = 8.0
@@ -77,7 +78,10 @@
     combined = residual.astype(jnp.float32) + returned.astype(jnp.float32)
     inv_rms = lax.rsqrt(jnp.mean(combined * combined, axis=2, keepdims=True) + epsilon)
     hidden = (combined * inv_rms * norm_gain).astype(jnp.bfloat16)
-    arrived = lax.all_gather(hidden, "vocab", axis=0, tiled=True)
+    w_next = tuple((hidden for _ in range(psum(1, axis_name="vocab"))))
+    t_next = jnp.stack(w_next, axis=0)
+    seen_now = all_to_all(t_next, axis_name="vocab", split_axis=0, concat_axis=0)
+    arrived = jnp.concatenate(seen_now, axis=0)
     row_count = arrived.shape[0]
     flattened = jnp.dot(
         arrived.reshape(row_count * docs_count, arrived.shape[2]),

time: 577 us -> 671 us (1.16)
  waiting for transfers between devices: 270 us -> 349 us
  local copies, waits for them, and re-layouts: 55.2 us -> 67.7 us
    all_to_all x0 -> x1, waiting for transfers between devices: none -> 143 us  [local(): all_to_all(t_next, axis_name='vocab', split_axis=0, concat_axis=0)]
    all_gather x1 -> x0, waiting for transfers between devices: 68.5 us -> none  [local(): arrived = lax.all_gather(hidden, 'vocab', axis=0, tiled=True)]
    all_to_all x0 -> x1, local copies, waits for them, and re-layouts: none -> 8.25 us  [local(): all_to_all(t_next, axis_name='vocab', split_axis=0, concat_axis=0)]
  transfers between devices with their start and end apart: 5 -> 5, of which waited for: 5 -> 5; matrix products, arithmetic and copies ran while one was open for 2% -> 1% of each run, Pallas kernels for 0% -> 0%
where the time goes in v1:
time: 671 us; the launch traced here: 670 us
  waiting for transfers between devices  349 us (52%)
  matrix products  140 us (21%)
  local copies, waits for them, and re-layouts  67.7 us (10%)
  blocking collectives  55.4 us (8%)
  other arithmetic  34 us (5%)
  between operations  14 us (2%)
  starting transfers between devices  9.1 us (1%)
    all_to_all x1, waiting for transfers between devices, local(): all_to_all(t_next, axis_name='vocab', split_axis=0, concat_axis=0)  143 us
    reduce_scatter x1, waiting for transfers between devices, local(): lax.psum_scatter(flattened.reshape(gathered_rows, docs_count, head_weight...  87.4 us
    all_gather x1, waiting for transfers between devices, local(): key_piece = lax.all_gather(key_heads, 'vocab', axis=0, tiled=True)  73.3 us
    dot_general x16, matrix products, attend_block(): jnp.einsum('bhqk,kbhe->qbhe', weights.astype(jnp.bfloat16), value_split,...  55.5 us
    dot_general x16, matrix products, attend_block(): jnp.einsum('qbhe,kbhe->bhqk', query_split, key_split, preferred_element_t...  48 us
    dynamic_slice x64, local copies, waits for them, and re-layouts, local(): lax.scan(attend_block, carry, (key_blocks, value_blocks, shards))  36.4 us
    all_gather x1, waiting for transfers between devices, local(): value_piece = lax.all_gather(value_heads, 'vocab', axis=0, tiled=True)  35 us
    dot_general x1, matrix products, local(): lax.dot_general(dlogits.reshape(gathered_rows * docs_count, dlogits.shape...  18.9 us
  transfers between devices with their start and end apart: 5, of which 5 were waited for; matrix products, arithmetic and copies ran while one was open for 1% of the time, Pallas kernels for 0%

profile of v1, /device:TPU:0, one launch (start us, length us, event | category | flops | bytes accessed | tf_op | source)
XLA Modules:
  0.0 670.1 jit_solution(5804131400767512240)
XLA Ops:
  10.6 14.7 %all_to_all.65 = bf16[8,2,16384]{2,1,0:T(2,128)(2,1)S(1)} all-to-all(bf16[8,2,16384]{2,1,0:T(2,128)(2,1)S(1)} %reshape.213), channel_id=1, replica_groups=mesh['seq'=8,'vocab'=16] {'seq'}, dimensions={0} | all-to-all | bytes 1048576 | tf_op jit(solution)/shard_map/all_to_all | solution.py:24
  31.2 12.8 %all_to_all.66 = bf16[8,2,16384]{2,1,0:T(2,128)(2,1)S(1)} all-to-all(bf16[8,2,16384]{2,1,0:T(2,128)(2,1)S(1)} %reshape.209), channel_id=1, replica_groups=mesh['seq'=8,'vocab'=16] {'seq'}, dimensions={0} | all-to-all | bytes 1048576 | tf_op jit(solution)/shard_map/all_to_all | solution.py:23
  49.0 3.5 all-to-all-start.1
  52.5 10.2 %all-to-all-done.1 = bf16[8,2,16384]{2,1,0:T(2,128)(2,1)S(1)} async-done(((bf16[8,2,16384]{2,1,0:T(2,128)(2,1)}), bf16[8,2,16384]{2,1,0:T(2,128)(2,1)S(1)}, u32[]{:S(2)}, u32[]{:S(2)}) %all-to-all-start.1) | async-done | bytes 524320 | tf_op jit(solution)/shard_map/all_to_all | solution.py:22
  64.3 35.0 %all-gather.5.cloned.1.call-done = bf16[8192,2,256]{2,0,1:T(8,128)(2,1)} async-done(((bf16[512,2,256]{2,0,1:T(8,128)(2,1)}), bf16[8192,2,256]{2,0,1:T(8,128)(2,1)}) %all-gather.5.cloned.1.call-update) | async-done | bytes 8388624 | tf_op jit(solution)/shard_map/all_gather | solution.py:65
  99.3 73.3 %all-gather.3.cloned.1.call-done = bf16[8192,2,256]{2,0,1:T(8,128)(2,1)} async-done(((bf16[512,2,256]{2,0,1:T(8,128)(2,1)}), bf16[8192,2,256]{2,0,1:T(8,128)(2,1)}) %all-gather.3.cloned.1.call-update) | async-done | bytes 8388624 | tf_op jit(solution)/shard_map/all_gather | solution.py:64
  172.6 168.3 %while.20 = (s32[]{:T(128)}, f32[2,2,512]{2,1,0:T(2,128)S(1)}, f32[2,2,512]{2,1,0:T(2,128)S(1)}, f32[512,2,2,128]{0,3,2,1:T(8,128)S(1)}, s32[16]{0:T(128)S(1)}, ...) while((s32[]{:T(128)}, f32[2,2,512]{2,1,0:T(2,128)S(1)}, ...), condition=%wide.region_3.4_spmd.clone.clone, body=%wide.region_0.3_spmd.clone.clone.sunk | while | flops 549213184 | bytes 37364912 | solution.py:70
  178.7 3.5 fusion.75
  186.0 3.0 select_reduce_fusion.2
  189.2 3.5 fusion.75
  196.5 3.0 select_reduce_fusion.2
  199.7 3.5 fusion.75
  207.0 3.0 select_reduce_fusion.2
  210.2 3.5 fusion.75
  217.5 3.0 select_reduce_fusion.2
  220.8 3.5 fusion.75
  228.0 3.0 select_reduce_fusion.2
  231.3 3.5 fusion.75
  238.6 3.0 select_reduce_fusion.2
  241.8 3.5 fusion.75
  249.1 3.0 select_reduce_fusion.2
  252.3 3.5 fusion.75
  259.6 3.0 select_reduce_fusion.2
  262.8 3.5 fusion.75
  270.1 3.0 select_reduce_fusion.2
  273.3 3.5 fusion.75
  280.6 3.0 select_reduce_fusion.2
  283.9 3.5 fusion.75
  291.1 3.0 select_reduce_fusion.2
  294.4 3.5 fusion.75
  301.7 3.0 select_reduce_fusion.2
  304.9 3.5 fusion.75
  312.2 3.0 select_reduce_fusion.2
  315.4 3.5 fusion.75
  322.7 3.0 select_reduce_fusion.2
  325.9 3.5 fusion.75
  333.2 3.0 select_reduce_fusion.2
  336.5 3.5 fusion.75
  341.5 14.5 %all_to_all.67 = bf16[512,2,256]{2,1,0:T(2,128)(2,1)S(1)} all-to-all(bf16[512,2,256]{2,1,0:T(2,128)(2,1)S(1)} %copy.93), channel_id=1, replica_groups=mesh['seq'=8,'vocab'=16] {'seq'}, dimensions={0} | all-to-all | bytes 1048576 | tf_op jit(solution)/shard_map/all_to_all | solution.py:77
  356.9 4.3 stack.2
  361.2 5.3 all-to-all-start.4
  366.8 143.0 %all-to-all-done.4 = bf16[16,64,2,2048]{3,1,2,0:T(8,128)(2,1)} async-done(((bf16[16,64,2,2048]{3,1,2,0:T(8,128)(2,1)}), bf16[16,64,2,2048]{3,1,2,0:T(8,128)(2,1)}, u32[]{:S(2)}, u32[]{:S(2)}) %all-to-all-start.4) | async-done | bytes 8388640 | tf_op jit(solution)/shard_map/all_to_all | solution.py:83
  509.8 8.3 %copy.85 = bf16[16,64,2,2048]{3,1,0,2:T(8,128)(2,1)} copy(bf16[16,64,2,2048]{3,1,2,0:T(8,128)(2,1)} %all-to-all-done.4) | data formatting | bytes 16777216 | tf_op jit(solution)/shard_map/all_to_all | solution.py:83
  518.0 17.6 %fusion.29 = (f32[2,1024]{1,0:T(2,128)S(1)}, f32[1024,2,1024]{2,0,1:T(8,128)}) fusion(f32[1024]{0:T(1024)S(1)} %copy-done.6, pred[1024,2]{0,1:T(4,128)(4,1)S(1)} %broadcast_compare_fusion.1, bf16[1024,2,2048]{2,0,1:T(8,128)(2,1)} %bitcast.86, bf16[2048,1024]{1,0:T(8,128)(2,1)} %param.15), kind=kOutput, calls=%fused_computation.44 | convolution fusion | flops 8600418304 | bytes 20985856 | tf_op jit(solution)/shard_map/dot_general | solution.py:86
  535.6 13.4 %psum.7 = f32[2,1024]{1,0:T(2,128)S(1)} all-reduce(f32[2,1024]{1,0:T(2,128)S(1)} %get-tuple-element.387), channel_id=1, replica_groups=mesh['seq'=8,'vocab'=16] {'seq'}, use_global_device_ids=true, to_apply=%region_6.7 | all-reduce | flops 2048 | bytes 16384 | tf_op jit(solution)/shard_map/psum | solution.py:102
  549.7 5.2 fusion.40
  554.9 18.9 %convolution_convert_fusion = bf16[1024,2,2048]{2,0,1:T(8,128)(2,1)} fusion(f32[1024,2,1024]{2,0,1:T(8,128)S(1)} %copy-done.1, bf16[2048,1024]{1,0:T(8,128)(2,1)} %param.15, f32[2,1024]{1,0:T(2,128)S(1)} %broadcast_divide_fusion, f32[1024]{0:T(1024)S(1)} %copy-done.6, pred[1024,2]{0,1:T(4,128)(4,1)S(1)} %broadcast_compare_fusion.1, ...), kind=kOutput, calls=%fused_computation.45 | convolution fusion | flops 8623489024 | bytes 22034432 | tf_op jit(solution)/shard_map/dot_general | solution.py:107
  573.9 87.4 %reduce-scatter.2.cloned.1.call-done = bf16[64,2,2048]{2,0,1:T(8,128)(2,1)} async-done(((bf16[1024,2,2048]{2,0,1:T(8,128)(2,1)}), bf16[64,2,2048]{2,0,1:T(8,128)(2,1)}) %reduce-scatter.2.cloned.1.call-update) | async-done | bytes 524304 | tf_op jit(solution)/shard_map/reduce_scatter | solution.py:113
  (260 shorter events, 87.4 us)
Async XLA Ops:
  7.2 39.4 %copy-start.3 = (bf16[64,2,2048]{2,1,0:T(2,128)(2,1)S(1)}, bf16[64,2,2048]{2,1,0:T(2,128)(2,1)}, u32[]{:S(2)}) copy-start(bf16[64,2,2048]{2,1,0:T(2,128)(2,1)} %param.10) | copy-start | bytes 1572868
  7.2 92.1 %all-gather.5.cloned.1.call-start = ((), (), s32[]{:S(2)}) async-start(), calls=%async_computation.7 | async-start | bytes 8912896 | tf_op jit(solution)/shard_map/all_gather | solution.py:65
  27.8 144.8 %copy-start.4 = (s32[2]{0:T(128)S(1)}, s32[2]{0:T(128)}, u32[]{:S(2)}) copy-start(s32[2]{0:T(128)} %param.17) | copy-start | bytes 28
  27.9 144.8 %all-gather.3.cloned.1.call-start = ((), (), s32[]{:S(2)}) async-start(), calls=%async_computation.6 | async-start | bytes 8912896 | tf_op jit(solution)/shard_map/all_gather | solution.py:64
  49.0 13.7 %all-to-all-start.1 = ((bf16[8,2,16384]{2,1,0:T(2,128)(2,1)}), bf16[8,2,16384]{2,1,0:T(2,128)(2,1)S(1)}, u32[]{:S(2)}, u32[]{:S(2)}) async-start(bf16[8,2,16384]{2,1,0:T(2,128)(2,1)} %reshape.211), calls=%async_computation.1 | async-start | bytes 1048576 | tf_op jit(solution)/shard_map/all_to_all | solution.py:22
  178.7 3.5 copy-start
  189.2 3.5 copy-start
  199.7 3.5 copy-start
  210.2 3.5 copy-start
  220.8 3.5 copy-start
  231.3 3.5 copy-start
  241.8 3.5 copy-start
  252.3 3.5 copy-start
  262.8 3.5 copy-start
  273.3 3.5 copy-start
  283.9 3.5 copy-start
  294.4 3.5 copy-start
  304.9 3.5 copy-start
  315.4 3.5 copy-start
  325.9 3.5 copy-start
  336.4 3.5 copy-start
  340.9 15.4 %copy-start.2 = (bf16[64,2,2048]{2,1,0:T(2,128)(2,1)S(1)}, bf16[64,2,2048]{2,1,0:T(2,128)(2,1)}, u32[]{:S(2)}) copy-start(bf16[64,2,2048]{2,1,0:T(2,128)(2,1)} %param.13) | copy-start | bytes 1572868
  340.9 15.7 %copy-start.5 = (f32[2048]{0:T(1024)S(1)}, f32[2048]{0:T(1024)}, u32[]{:S(2)}) copy-start(f32[2048]{0:T(1024)} %param.14) | copy-start | bytes 24580
  361.2 148.6 %all-to-all-start.4 = ((bf16[16,64,2,2048]{3,1,2,0:T(8,128)(2,1)}), bf16[16,64,2,2048]{3,1,2,0:T(8,128)(2,1)}, u32[]{:S(2)}, u32[]{:S(2)}) async-start(bf16[16,64,2,2048]{3,1,2,0:T(8,128)(2,1)} %stack.2), calls=%async_computation.4 | async-start | bytes 16777216 | tf_op jit(solution)/shard_map/all_to_all | solution.py:83
  366.5 294.8 %reduce-scatter.2.cloned.1.call-start = ((), (), s32[]{:S(2)}) async-start(), calls=%async_computation.8 | async-start | bytes 8912896 | tf_op jit(solution)/shard_map/reduce_scatter | solution.py:113
  366.8 151.2 %copy-start.6 = (f32[1024]{0:T(1024)S(1)}, f32[1024]{0:T(1024)}, u32[]{:S(2)}) copy-start(f32[1024]{0:T(1024)} %param.16) | copy-start | bytes 12292
  549.0 5.9 copy-start.1
Sparse Core Ops, SparseCore 0:
  28.0 71.2 all-gather.4
  102.1 70.5 all-gather.2
  574.0 87.1 reduce-scatter.1
